TPU v7x, 512 devices: a whole 4x4x16 slice. The times are simulated.
512 devices in a mesh: sector: 16 (over y, x_lo, core), dom: 32 (over z, x_hi).
Axes of the slice: x: 4 (x_hi: 2, x_lo: 2; x = x_hi * 2 + x_lo), y: 4, z: 16, core: 2. Of those that a mesh axis runs over, the one named last changes fastest.
Arguments:
- amplitudes: float32 [64, 48], replicated, may hold values from -0.3 to 0.3
- mode_shapes: float32 [48, 3, 524288], P(None, None, ('sector', 'dom')), may hold values from -6 to 6
- shape_grads: float32 [8, 3, 524288], P(None, None, ('sector', 'dom')), may hold values from -2.4 to 2.4
- lame_params: float32 [2, 524288], P(None, ('sector', 'dom')), may hold values from 0.5 to 2
- connectivity: int32 [8, 524288], P(None, ('sector', 'dom')), may hold values from -1 to 1791, as said below
- dom_sends: int32 [2, 131072], P(None, ('sector', 'dom')), may hold values from -1 to 1023, as said below
- sector_sends: int32 [2, 65536], P(None, ('sector', 'dom')), may hold values from -1 to 1023, as said below
Outputs:
- nodal_force: float32 [64, 3, 524288], P(None, None, ('sector', 'dom'))
- modal_force: float32 [64, 48], replicated
Inputs may be any that keep to these rules, and one draw needn't show every extreme that they name: `connectivity`: in each device's block, the live elements come first and the padding element slots after them hold -1 in all 8 rows; a live slot names a slot of the device's extended table. Some device has all 1024 slots live. `dom_sends`: each device's row lists its own node numbers first, then -1; a row holds 128 to 256 live entries, and some row is full. `sector_sends`: each device's row lists its own node numbers first, then -1; a row holds 64 to 128 live entries, and some row is full.
All inputs are finite; a program needn't handle non-finite values.
Results may differ from a plain program's by a relative error of at most 0.0003.
Values sent between devices are 32-bit elements; how exact they have to be, the bound alone decides.
A program may use at most 64 MiB of HBM per device.

v0:
```python
import math
import jax
import jax.numpy as jnp
from jax import lax
from jax.sharding import PartitionSpec as P


def padded(cells, sides, width, closed):
    for axis, dim in sides:
        count = lax.axis_size(axis)
        ends = count if closed else count - 1
        head = lax.slice_in_dim(cells, 0, width, axis=dim)
        tail = lax.slice_in_dim(cells, cells.shape[dim] - width, cells.shape[dim], axis=dim)
        cells = jnp.concatenate(
            [
                lax.ppermute(tail, axis, [(i, (i + 1) % count) for i in range(ends)]),
                cells,
                lax.ppermute(head, axis, [((i + 1) % count, i) for i in range(ends)]),
            ],
            axis=dim,
        )
    return cells


def take_slots(node_table, send_lists):
    slot_width = node_table.shape[1]
    slot_index = jnp.where(send_lists < 0, slot_width, send_lists).reshape(-1)
    return jnp.take(node_table, slot_index, axis=1, mode="fill", fill_value=0.0)


def add_slots(node_table, send_lists, add_values):
    slot_width = node_table.shape[1]
    slot_index = jnp.where(send_lists < 0, slot_width, send_lists).reshape(-1)
    return node_table.at[:, slot_index].add(add_values, mode="drop")


def element_forces(accum, extended, connect, gradients, lame):
    ext_width = extended.shape[1]
    combo_total = extended.shape[0] // 3
    elem_total = connect.shape[1]
    slot_index = jnp.where(connect < 0, ext_width, connect).reshape(-1)
    corners = jnp.take(extended, slot_index, axis=1, mode="fill", fill_value=0.0).reshape(
        combo_total, 3, 8, elem_total
    )
    gradient = jnp.zeros((combo_total, 3, 3, elem_total), extended.dtype)
    for corner in range(8):
        gradient = gradient + corners[:, :, None, corner, :] * gradients[corner][None, None, :, :]
    quadratic = jnp.sum(gradient[:, :, :, None, :] * gradient[:, :, None, :, :], axis=1)
    green_strain = 0.5 * (gradient + jnp.swapaxes(gradient, 1, 2) + quadratic)
    strain_trace = green_strain[:, 0, 0] + green_strain[:, 1, 1] + green_strain[:, 2, 2]
    identity = jnp.eye(3, dtype=extended.dtype)[None, :, :, None]
    stress = lame[0] * strain_trace[:, None, None, :] * identity + 2.0 * lame[1] * green_strain
    piola = stress + jnp.sum(gradient[:, :, :, None, :] * stress[:, None, :, :, :], axis=2)
    corner_forces = jnp.stack(
        [jnp.sum(piola * gradients[corner][None, None, :, :], axis=2) for corner in range(8)],
        axis=2,
    )
    return accum.at[:, slot_index].add(
        corner_forces.reshape(3 * combo_total, 8 * elem_total), mode="drop"
    )


def outer_ends(ext_rows, slot_width):
    return jnp.concatenate([ext_rows[:, :slot_width], ext_rows[:, 3 * slot_width :]], axis=1)


def local(amplitudes, mode_shapes, shape_grads, lame_params, connectivity, dom_sends, sector_sends):
    modes_total, _, node_total = mode_shapes.shape
    combo_total = amplitudes.shape[0]
    table_rows = 3 * combo_total
    dom_width = dom_sends.shape[1]
    sec_width = sector_sends.shape[1]
    flat_shapes = mode_shapes.reshape(modes_total, 3 * node_total)
    displaced = jnp.dot(
        amplitudes, flat_shapes, precision=lax.Precision.HIGHEST, preferred_element_type=jnp.float32
    ).reshape(table_rows, node_total)
    dom_ext = padded(take_slots(displaced, dom_sends), (("dom", 1),), dom_width, False)
    sec_ext = padded(take_slots(displaced, sector_sends), (("sector", 1),), sec_width, True)
    halo_moved = jnp.concatenate(
        [outer_ends(dom_ext, dom_width), outer_ends(sec_ext, sec_width)], axis=1
    )
    extended = jnp.concatenate([displaced, halo_moved], axis=1)
    ext_width = extended.shape[1]
    elem_total = connectivity.shape[1]
    block_size = math.gcd(elem_total, 256)
    turn_total = elem_total // block_size

    def one_block(turn_index, forces):
        first_col = turn_index * block_size
        connect_block = lax.dynamic_slice_in_dim(connectivity, first_col, block_size, 1)
        grads_block = lax.dynamic_slice_in_dim(shape_grads, first_col, block_size, 2)
        lame_block = lax.dynamic_slice_in_dim(lame_params, first_col, block_size, 1)
        return element_forces(forces, extended, connect_block, grads_block, lame_block)

    slot_forces = lax.fori_loop(
        0, turn_total, one_block, jnp.zeros((table_rows, ext_width), jnp.float32)
    )
    own_forces = slot_forces[:, :node_total]
    dom_back = slot_forces[:, node_total : node_total + 2 * dom_width]
    sec_back = slot_forces[:, node_total + 2 * dom_width :]
    dom_return = padded(dom_back, (("dom", 1),), dom_width, False)
    own_forces = add_slots(own_forces, dom_sends, outer_ends(dom_return, dom_width))
    sec_return = padded(sec_back, (("sector", 1),), sec_width, True)
    own_forces = add_slots(own_forces, sector_sends, outer_ends(sec_return, sec_width))
    partial_modal = lax.dot_general(
        own_forces.reshape(combo_total, 3 * node_total),
        flat_shapes,
        (((1,), (1,)), ((), ())),
        precision=lax.Precision.HIGHEST,
        preferred_element_type=jnp.float32,
    )
    modal_total = lax.psum(partial_modal, ("sector", "dom"))
    all_nodes = node_total * lax.axis_size("sector") * lax.axis_size("dom")
    return (
        own_forces.reshape(combo_total, 3, node_total),
        modal_total / math.sqrt(3.0 * all_nodes),
    )


def solution(mesh):
    placed = (
        P(),
        P(None, None, ("sector", "dom")),
        P(None, None, ("sector", "dom")),
        P(None, ("sector", "dom")),
        P(None, ("sector", "dom")),
        P(None, ("sector", "dom")),
        P(None, ("sector", "dom")),
    )
    return jax.shard_map(
        local,
        mesh=mesh,
        in_specs=placed,
        out_specs=(P(None, None, ("sector", "dom")), P()),
        check_vma=False,
    )
```

profile of v0, /device:TPU:1, one launch (start us, length us, event | category | flops | bytes accessed | tf_op | source)
XLA Modules:
  0.0 308.0 jit_solution(2652404135059010113)
XLA Ops:
  0.6 0.7 compare_select_fusion.8
  1.3 0.7 fusion.11
  2.1 1.1 copy.105
  3.2 0.8 copy-done.2
  4.0 0.8 fusion.17
  5.3 1.6 gather_fusion.1
  7.1 5.5 %collective-permute-start = (f32[192,256]{0,1:T(8,128)S(1)}, f32[192,256]{0,1:T(8,128)S(1)}, u32[]{:S(2)}, u32[]{:S(2)}) collective-permute-start(f32[192,256]{0,1:T(8,128)S(1)} %get-tuple-element.244), channel_id=1, source_target_pairs={{0,1},{1,2},{2,3},{3,4},{4,5},{5,6},{6,7},{7,8},{8,9},{9,10},{10,1... | collective-permute-start | bytes 589832 | tf_op jit(solution)/shard_map/ppermute | solution.py:16
  12.6 1.0 gather_fusion.2
  13.7 4.6 %collective-permute-start.3 = (f32[192,128]{0,1:T(8,128)S(1)}, f32[192,128]{0,1:T(8,128)S(1)}, u32[]{:S(2)}, u32[]{:S(2)}) collective-permute-start(f32[192,128]{0,1:T(8,128)S(1)} %get-tuple-element.245), channel_id=1, source_target_pairs={{32,0},{64,32},{96,64},{128,96},{160,128},{192,160},{224,192},{256... | collective-permute-start | bytes 294920 | tf_op jit(solution)/shard_map/ppermute | solution.py:18
  18.4 1.9 collective-permute-start.2
  20.3 1.5 collective-permute-start.1
  21.9 9.2 %collective-permute-done.1 = f32[192,256]{0,1:T(8,128)S(1)} collective-permute-done((f32[192,256]{0,1:T(8,128)S(1)}, f32[192,256]{0,1:T(8,128)S(1)}, u32[]{:S(2)}, u32[]{:S(2)}) %collective-permute-start.1) | collective-permute-done | bytes 196640 | tf_op jit(solution)/shard_map/ppermute | solution.py:18
  31.3 1.1 copy-done.1
  32.4 136.4 %while.15 = (s32[]{:T(128)}, f32[192,1792]{0,1:T(8,128)S(1)}, s32[8,1024]{1,0:T(8,128)S(1)}, f32[2,1024]{1,0:T(2,128)}, f32[192,1792]{0,1:T(8,128)}, /*index=5*/...) while((s32[]{:T(128)}, f32[192,1792]{0,1:T(8,128)S(1)}, ...), condition=%wide.region_12.13_spmd, body=%wide.region_0.12_spmd.sunk | while | flops 12415007 | bytes 49229240 | solution.py:95
  32.4 0.8 constant_dynamic-slice_fusion.12
  33.3 1.3 constant_dynamic-slice_fusion.11
  34.6 10.1 %gather_fusion = f32[2048,192]{1,0:T(8,128)} fusion(f32[192,1792]{0,1:T(8,128)} %get-tuple-element.414, s32[2048]{0:T(1024)S(1)} %broadcast_clamp_fusion.2), kind=kCustom, calls=%fused_computation.clone.1 | custom fusion | bytes 3153920 | tf_op jit(solution)/shard_map/while/body/eval_jaxpr/jit(_take)/gather | solution.py:42
  44.7 1.9 copy.147
  46.6 0.6 copy.148
  47.3 1.1 fusion.28
  50.4 0.9 copy.149
  51.9 1.8 copy.151
  53.8 12.6 %scatter_fusion = f32[192,1792]{0,1:T(8,128)S(1)} fusion(f32[192,1792]{0,1:T(8,128)S(1)} %get-tuple-element.394, s32[2048]{0:T(1024)S(1)} %bitcast.158, f32[2048,192]{1,0:T(8,128)} %copy.151), kind=kCustom, calls=%fused_computation.3.clone.1 | custom fusion | flops 393216 | bytes 4726784 | tf_op jit(solution)/shard_map/while/body/eval_jaxpr/scatter-add | solution.py:58
  66.5 0.8 constant_dynamic-slice_fusion.12
  67.4 1.4 constant_dynamic-slice_fusion.11
  68.8 10.1 %gather_fusion = f32[2048,192]{1,0:T(8,128)} fusion(f32[192,1792]{0,1:T(8,128)} %get-tuple-element.414, s32[2048]{0:T(1024)S(1)} %broadcast_clamp_fusion.2), kind=kCustom, calls=%fused_computation.clone.1 | custom fusion | bytes 3153920 | tf_op jit(solution)/shard_map/while/body/eval_jaxpr/jit(_take)/gather | solution.py:42
  78.8 1.9 copy.147
  81.4 1.1 fusion.28
  84.5 0.9 copy.149
  86.0 1.8 copy.151
  87.9 12.6 %scatter_fusion = f32[192,1792]{0,1:T(8,128)S(1)} fusion(f32[192,1792]{0,1:T(8,128)S(1)} %get-tuple-element.394, s32[2048]{0:T(1024)S(1)} %bitcast.158, f32[2048,192]{1,0:T(8,128)} %copy.151), kind=kCustom, calls=%fused_computation.3.clone.1 | custom fusion | flops 393216 | bytes 4726784 | tf_op jit(solution)/shard_map/while/body/eval_jaxpr/scatter-add | solution.py:58
  100.6 0.8 constant_dynamic-slice_fusion.12
  101.5 1.3 constant_dynamic-slice_fusion.11
  102.8 10.1 %gather_fusion = f32[2048,192]{1,0:T(8,128)} fusion(f32[192,1792]{0,1:T(8,128)} %get-tuple-element.414, s32[2048]{0:T(1024)S(1)} %broadcast_clamp_fusion.2), kind=kCustom, calls=%fused_computation.clone.1 | custom fusion | bytes 3153920 | tf_op jit(solution)/shard_map/while/body/eval_jaxpr/jit(_take)/gather | solution.py:42
  112.9 1.9 copy.147
  114.8 0.6 copy.148
  115.5 1.1 fusion.28
  118.6 0.9 copy.149
  119.5 0.6 copy.150
  120.1 1.8 copy.151
  122.0 12.6 %scatter_fusion = f32[192,1792]{0,1:T(8,128)S(1)} fusion(f32[192,1792]{0,1:T(8,128)S(1)} %get-tuple-element.394, s32[2048]{0:T(1024)S(1)} %bitcast.158, f32[2048,192]{1,0:T(8,128)} %copy.151), kind=kCustom, calls=%fused_computation.3.clone.1 | custom fusion | flops 393216 | bytes 4726784 | tf_op jit(solution)/shard_map/while/body/eval_jaxpr/scatter-add | solution.py:58
  134.7 0.8 constant_dynamic-slice_fusion.12
  135.6 1.4 constant_dynamic-slice_fusion.11
  137.0 10.1 %gather_fusion = f32[2048,192]{1,0:T(8,128)} fusion(f32[192,1792]{0,1:T(8,128)} %get-tuple-element.414, s32[2048]{0:T(1024)S(1)} %broadcast_clamp_fusion.2), kind=kCustom, calls=%fused_computation.clone.1 | custom fusion | bytes 3153920 | tf_op jit(solution)/shard_map/while/body/eval_jaxpr/jit(_take)/gather | solution.py:42
  147.0 1.9 copy.147
  148.9 0.6 copy.148
  149.6 1.1 fusion.28
  152.7 0.9 copy.149
  153.6 0.6 copy.150
  154.2 1.8 copy.151
  156.1 12.6 %scatter_fusion = f32[192,1792]{0,1:T(8,128)S(1)} fusion(f32[192,1792]{0,1:T(8,128)S(1)} %get-tuple-element.394, s32[2048]{0:T(1024)S(1)} %bitcast.158, f32[2048,192]{1,0:T(8,128)} %copy.151), kind=kCustom, calls=%fused_computation.3.clone.1 | custom fusion | flops 393216 | bytes 4726784 | tf_op jit(solution)/shard_map/while/body/eval_jaxpr/scatter-add | solution.py:58
  168.8 2.8 collective-permute-start.4
  171.6 1.3 collective-permute-start.5
  172.9 0.7 fusion.13
  173.6 4.8 %collective-permute-start.6 = (f32[192,128]{0,1:T(8,128)}, f32[192,128]{0,1:T(8,128)}, u32[]{:S(2)}, u32[]{:S(2)}) collective-permute-start(f32[192,128]{0,1:T(8,128)} %get-tuple-element.239), channel_id=1, source_target_pairs={{0,32},{32,64},{64,96},{96,128},{128,160},{160,192},{192,224},{224... | collective-permute-start | bytes 294920 | tf_op jit(solution)/shard_map/ppermute | solution.py:16
  178.4 2.2 collective-permute-start.7
  180.7 3.8 %scatter_custom_fusion.1 = f32[192,1024]{0,1:T(8,128)S(1)} fusion(f32[192,1024]{0,1:T(8,128)S(1)} %slice.257, s32[512]{0:T(512)S(1)} %bitcast.167, f32[192,256]{0,1:T(8,128)S(1)} %collective-permute-done.5, f32[]{:T(128)} %constant.154, f32[192,256]{0,1:T(8,128)S(1)} %collective-permute-done.4), kind=kCustom, calls=%fused_computation.67 | custom fusion | flops 196608 | bytes 1310724 | tf_op jit(solution)/shard_map/scatter-add | solution.py:34
  184.5 0.9 collective-permute-done.6
  185.4 4.3 %collective-permute-done.7 = f32[192,128]{0,1:T(8,128)} collective-permute-done((f32[192,128]{0,1:T(8,128)}, f32[192,128]{0,1:T(8,128)}, u32[]{:S(2)}, u32[]{:S(2)}) %collective-permute-start.7) | collective-permute-done | bytes 98336 | tf_op jit(solution)/shard_map/ppermute | solution.py:18
  189.6 3.0 scatter_custom_fusion.2
  194.1 0.8 fusion.18
  194.8 111.2 %psum.7 = f32[64,48]{0,1:T(8,128)S(1)} all-reduce(f32[64,48]{0,1:T(8,128)S(1)} %fusion.18), channel_id=1, replica_groups=mesh['sector'=16,'dom'=32] {'sector','dom'}, use_global_device_ids=true, to_apply=%region_15.16 | all-reduce | flops 3072 | bytes 24576 | tf_op jit(solution)/shard_map/psum | solution.py:112
  306.0 0.6 broadcast_multiply_fusion.1
  306.6 1.3 copy.92
  (162 shorter events, 12.6 us)
Async XLA Ops:
  0.6 3.4 %copy-start = (f32[64,48]{0,1:T(8,128)S(1)}, f32[64,48]{0,1:T(8,128)}, u32[]{:S(2)}) copy-start(f32[64,48]{0,1:T(8,128)} %param.9) | copy-start | bytes 36868
  3.2 0.8 copy-start.2
  6.9 5.7 %copy-start.5 = (s32[2,128]{1,0:T(2,128)S(1)}, s32[2,128]{1,0:T(2,128)}, u32[]{:S(2)}) copy-start(s32[2,128]{1,0:T(2,128)} %param.15) | copy-start | bytes 3076
  7.1 14.8 %collective-permute-start = (f32[192,256]{0,1:T(8,128)S(1)}, f32[192,256]{0,1:T(8,128)S(1)}, u32[]{:S(2)}, u32[]{:S(2)}) collective-permute-start(f32[192,256]{0,1:T(8,128)S(1)} %get-tuple-element.244), channel_id=1, source_target_pairs={{0,1},{1,2},{2,3},{3,4},{4,5},{5,6},{6,7},{7,8},{8,9},{9,10},{10,1... | collective-permute-start | bytes 589832 | tf_op jit(solution)/shard_map/ppermute | solution.py:16
  13.7 17.4 %collective-permute-start.3 = (f32[192,128]{0,1:T(8,128)S(1)}, f32[192,128]{0,1:T(8,128)S(1)}, u32[]{:S(2)}, u32[]{:S(2)}) collective-permute-start(f32[192,128]{0,1:T(8,128)S(1)} %get-tuple-element.245), channel_id=1, source_target_pairs={{32,0},{64,32},{96,64},{128,96},{160,128},{192,160},{224,192},{256... | collective-permute-start | bytes 294920 | tf_op jit(solution)/shard_map/ppermute | solution.py:18
  18.4 12.7 %collective-permute-start.2 = (f32[192,128]{0,1:T(8,128)S(1)}, f32[192,128]{0,1:T(8,128)S(1)}, u32[]{:S(2)}, u32[]{:S(2)}) collective-permute-start(f32[192,128]{0,1:T(8,128)S(1)} %get-tuple-element.246), channel_id=1, source_target_pairs={{0,32},{32,64},{64,96},{96,128},{128,160},{160,192},{192,224},{224... | collective-permute-start | bytes 294920 | tf_op jit(solution)/shard_map/ppermute | solution.py:16
  20.3 10.8 %collective-permute-start.1 = (f32[192,256]{0,1:T(8,128)S(1)}, f32[192,256]{0,1:T(8,128)S(1)}, u32[]{:S(2)}, u32[]{:S(2)}) collective-permute-start(f32[192,256]{0,1:T(8,128)S(1)} %get-tuple-element.243), channel_id=1, source_target_pairs={{1,0},{2,1},{3,2},{4,3},{5,4},{6,5},{7,6},{8,7},{9,8},{10,9},{11,1... | collective-permute-start | bytes 589832 | tf_op jit(solution)/shard_map/ppermute | solution.py:18
  21.9 10.5 %copy-start.4 = (s32[8,1024]{1,0:T(8,128)S(1)}, s32[8,1024]{1,0:T(8,128)}, u32[]{:S(2)}) copy-start(s32[8,1024]{1,0:T(8,128)} %param.13) | copy-start | bytes 98308
  31.1 1.2 copy-start.1
  168.8 11.9 %collective-permute-start.4 = (f32[192,256]{0,1:T(8,128)S(1)}, f32[192,256]{0,1:T(8,128)S(1)}, u32[]{:S(2)}, u32[]{:S(2)}) collective-permute-start(f32[192,256]{0,1:T(8,128)S(1)} %get-tuple-element.241), channel_id=1, source_target_pairs={{0,1},{1,2},{2,3},{3,4},{4,5},{5,6},{6,7},{7,8},{8,9},{9,10},{10,1... | collective-permute-start | bytes 589832 | tf_op jit(solution)/shard_map/ppermute | solution.py:16
  171.6 9.1 %collective-permute-start.5 = (f32[192,256]{0,1:T(8,128)S(1)}, f32[192,256]{0,1:T(8,128)S(1)}, u32[]{:S(2)}, u32[]{:S(2)}) collective-permute-start(f32[192,256]{0,1:T(8,128)S(1)} %get-tuple-element.242), channel_id=1, source_target_pairs={{1,0},{2,1},{3,2},{4,3},{5,4},{6,5},{7,6},{8,7},{9,8},{10,9},{11,1... | collective-permute-start | bytes 589832 | tf_op jit(solution)/shard_map/ppermute | solution.py:18
  173.6 11.8 %collective-permute-start.6 = (f32[192,128]{0,1:T(8,128)}, f32[192,128]{0,1:T(8,128)}, u32[]{:S(2)}, u32[]{:S(2)}) collective-permute-start(f32[192,128]{0,1:T(8,128)} %get-tuple-element.239), channel_id=1, source_target_pairs={{0,32},{32,64},{64,96},{96,128},{128,160},{160,192},{192,224},{224... | collective-permute-start | bytes 294920 | tf_op jit(solution)/shard_map/ppermute | solution.py:16
  178.4 11.3 %collective-permute-start.7 = (f32[192,128]{0,1:T(8,128)}, f32[192,128]{0,1:T(8,128)}, u32[]{:S(2)}, u32[]{:S(2)}) collective-permute-start(f32[192,128]{0,1:T(8,128)} %get-tuple-element.240), channel_id=1, source_target_pairs={{32,0},{64,32},{96,64},{128,96},{160,128},{192,160},{224,192},{256... | collective-permute-start | bytes 294920 | tf_op jit(solution)/shard_map/ppermute | solution.py:18
  193.0 1.1 copy-start.3
where the time goes:
time: 309 us; the launch traced here: 308 us
  blocking collectives  111 us (36%)
  local copies, waits for them, and re-layouts  87.5 us (28%)
  other arithmetic  66.7 us (22%)
  starting transfers between devices  24.6 us (8%)
  waiting for transfers between devices  14.3 us (5%)
    psum x1, blocking collectives, local(): modal_total = lax.psum(partial_modal, ('sector', 'dom'))  111 us
    scatter-add x4, other arithmetic, element_forces(): accum.at[:, slot_index]  50.6 us
    gather x8, local copies, waits for them, and re-layouts, element_forces(): jnp.take(extended, slot_index, axis=1, mode='fill', fill_value=0.0)  47.8 us
    ppermute x4, starting transfers between devices, padded(): lax.ppermute(tail, axis, [(i, (i + 1) % count) for i in range(ends)])  15 us
    ppermute x4, waiting for transfers between devices, padded(): lax.ppermute(head, axis, [((i + 1) % count, i) for i in range(ends)])  13.4 us
    ppermute x4, starting transfers between devices, padded(): lax.ppermute(head, axis, [((i + 1) % count, i) for i in range(ends)])  9.62 us
    reshape x4, local copies, waits for them, and re-layouts, element_forces(): corner_forces.reshape(3 * combo_total, 8 * elem_total)  7.39 us
    scatter-add x2, other arithmetic, add_slots(): return node_table.at[:, slot_index].add(add_values, mode='drop')  6.78 us
  transfers between devices with their start and end apart: 8, of which 3 were waited for; matrix products, arithmetic and copies ran while one was open for 2% of the time, Pallas kernels for 0%

commit v1 on v0

--- a/solution.py
+++ b/solution.py
@@ -109,7 +109,7 @@
         precision=lax.Precision.HIGHEST,
         preferred_element_type=jnp.float32,
     )
-    modal_total = lax.psum(partial_modal, ("sector", "dom"))
+    modal_total = lax.psum(lax.psum(partial_modal, "sector"), "dom")
     all_nodes = node_total * lax.axis_size("sector") * lax.axis_size("dom")
     return (
         own_forces.reshape(combo_total, 3, node_total),

time: 309 us -> 403 us (1.30)
  the two profiles are of different devices: /device:TPU:1 before, /device:TPU:32 now
where the time goes in v1:
time: 403 us; the launch traced here: 401 us
  blocking collectives  204 us (51%)
  local copies, waits for them, and re-layouts  87.5 us (22%)
  other arithmetic  66.7 us (17%)
  starting transfers between devices  31.9 us (8%)
  waiting for transfers between devices  7.5 us (2%)
    psum x2, blocking collectives, local(): modal_total = lax.psum(lax.psum(partial_modal, 'sector'), 'dom')  204 us
    scatter-add x4, other arithmetic, element_forces(): accum.at[:, slot_index]  50.6 us
    gather x8, local copies, waits for them, and re-layouts, element_forces(): jnp.take(extended, slot_index, axis=1, mode='fill', fill_value=0.0)  47.8 us
    ppermute x4, starting transfers between devices, padded(): lax.ppermute(head, axis, [((i + 1) % count, i) for i in range(ends)])  17.9 us
    ppermute x4, starting transfers between devices, padded(): lax.ppermute(tail, axis, [(i, (i + 1) % count) for i in range(ends)])  13.9 us
  transfers between devices with their start and end apart: 8, of which 3 were waited for; matrix products, arithmetic and copies ran while one was open for 1% of the time, Pallas kernels for 0%

profile of v1, /device:TPU:32, one launch (start us, length us, event | category | flops | bytes accessed | tf_op | source)
XLA Modules:
  0.0 401.2 jit_solution(17959535056522913990)
XLA Ops:
  0.6 0.7 compare_select_fusion.8
  1.3 0.7 fusion.11
  2.1 1.1 copy.105
  3.2 0.8 copy-done.2
  4.0 0.8 fusion.17
  5.3 1.6 gather_fusion.1
  7.1 4.9 %collective-permute-start = (f32[192,256]{0,1:T(8,128)S(1)}, f32[192,256]{0,1:T(8,128)S(1)}, u32[]{:S(2)}, u32[]{:S(2)}) collective-permute-start(f32[192,256]{0,1:T(8,128)S(1)} %get-tuple-element.244), channel_id=1, source_target_pairs={{0,1},{1,2},{2,3},{3,4},{4,5},{5,6},{6,7},{7,8},{8,9},{9,10},{10,1... | collective-permute-start | bytes 589832 | tf_op jit(solution)/shard_map/ppermute | solution.py:16
  12.1 1.0 gather_fusion.2
  13.2 4.1 %collective-permute-start.3 = (f32[192,128]{0,1:T(8,128)S(1)}, f32[192,128]{0,1:T(8,128)S(1)}, u32[]{:S(2)}, u32[]{:S(2)}) collective-permute-start(f32[192,128]{0,1:T(8,128)S(1)} %get-tuple-element.245), channel_id=1, source_target_pairs={{32,0},{64,32},{96,64},{128,96},{160,128},{192,160},{224,192},{256... | collective-permute-start | bytes 294920 | tf_op jit(solution)/shard_map/ppermute | solution.py:18
  17.3 1.9 collective-permute-start.2
  19.2 5.0 %collective-permute-start.1 = (f32[192,256]{0,1:T(8,128)S(1)}, f32[192,256]{0,1:T(8,128)S(1)}, u32[]{:S(2)}, u32[]{:S(2)}) collective-permute-start(f32[192,256]{0,1:T(8,128)S(1)} %get-tuple-element.243), channel_id=1, source_target_pairs={{1,0},{2,1},{3,2},{4,3},{5,4},{6,5},{7,6},{8,7},{9,8},{10,9},{11,1... | collective-permute-start | bytes 589832 | tf_op jit(solution)/shard_map/ppermute | solution.py:18
  24.4 6.0 %collective-permute-done.1 = f32[192,256]{0,1:T(8,128)S(1)} collective-permute-done((f32[192,256]{0,1:T(8,128)S(1)}, f32[192,256]{0,1:T(8,128)S(1)}, u32[]{:S(2)}, u32[]{:S(2)}) %collective-permute-start.1) | collective-permute-done | bytes 196640 | tf_op jit(solution)/shard_map/ppermute | solution.py:18
  30.6 1.1 copy-done.1
  31.7 136.4 %while.15 = (s32[]{:T(128)}, f32[192,1792]{0,1:T(8,128)S(1)}, s32[8,1024]{1,0:T(8,128)S(1)}, f32[2,1024]{1,0:T(2,128)}, f32[192,1792]{0,1:T(8,128)}, /*index=5*/...) while((s32[]{:T(128)}, f32[192,1792]{0,1:T(8,128)S(1)}, ...), condition=%wide.region_12.13_spmd, body=%wide.region_0.12_spmd.sunk | while | flops 12415007 | bytes 49229240 | solution.py:95
  31.7 0.8 constant_dynamic-slice_fusion.12
  32.6 1.3 constant_dynamic-slice_fusion.11
  33.9 10.1 %gather_fusion = f32[2048,192]{1,0:T(8,128)} fusion(f32[192,1792]{0,1:T(8,128)} %get-tuple-element.414, s32[2048]{0:T(1024)S(1)} %broadcast_clamp_fusion.2), kind=kCustom, calls=%fused_computation.clone.1 | custom fusion | bytes 3153920 | tf_op jit(solution)/shard_map/while/body/eval_jaxpr/jit(_take)/gather | solution.py:42
  44.0 1.9 copy.147
  45.9 0.6 copy.148
  46.6 1.1 fusion.28
  49.7 0.9 copy.149
  51.2 1.8 copy.151
  53.1 12.6 %scatter_fusion = f32[192,1792]{0,1:T(8,128)S(1)} fusion(f32[192,1792]{0,1:T(8,128)S(1)} %get-tuple-element.394, s32[2048]{0:T(1024)S(1)} %bitcast.158, f32[2048,192]{1,0:T(8,128)} %copy.151), kind=kCustom, calls=%fused_computation.3.clone.1 | custom fusion | flops 393216 | bytes 4726784 | tf_op jit(solution)/shard_map/while/body/eval_jaxpr/scatter-add | solution.py:58
  65.8 0.8 constant_dynamic-slice_fusion.12
  66.7 1.4 constant_dynamic-slice_fusion.11
  68.1 10.1 %gather_fusion = f32[2048,192]{1,0:T(8,128)} fusion(f32[192,1792]{0,1:T(8,128)} %get-tuple-element.414, s32[2048]{0:T(1024)S(1)} %broadcast_clamp_fusion.2), kind=kCustom, calls=%fused_computation.clone.1 | custom fusion | bytes 3153920 | tf_op jit(solution)/shard_map/while/body/eval_jaxpr/jit(_take)/gather | solution.py:42
  78.1 1.9 copy.147
  80.7 1.1 fusion.28
  83.8 0.9 copy.149
  85.3 1.8 copy.151
  87.2 12.6 %scatter_fusion = f32[192,1792]{0,1:T(8,128)S(1)} fusion(f32[192,1792]{0,1:T(8,128)S(1)} %get-tuple-element.394, s32[2048]{0:T(1024)S(1)} %bitcast.158, f32[2048,192]{1,0:T(8,128)} %copy.151), kind=kCustom, calls=%fused_computation.3.clone.1 | custom fusion | flops 393216 | bytes 4726784 | tf_op jit(solution)/shard_map/while/body/eval_jaxpr/scatter-add | solution.py:58
  99.9 0.8 constant_dynamic-slice_fusion.12
  100.8 1.3 constant_dynamic-slice_fusion.11
  102.1 10.1 %gather_fusion = f32[2048,192]{1,0:T(8,128)} fusion(f32[192,1792]{0,1:T(8,128)} %get-tuple-element.414, s32[2048]{0:T(1024)S(1)} %broadcast_clamp_fusion.2), kind=kCustom, calls=%fused_computation.clone.1 | custom fusion | bytes 3153920 | tf_op jit(solution)/shard_map/while/body/eval_jaxpr/jit(_take)/gather | solution.py:42
  112.2 1.9 copy.147
  114.1 0.6 copy.148
  114.8 1.1 fusion.28
  117.9 0.9 copy.149
  118.8 0.6 copy.150
  119.4 1.8 copy.151
  121.3 12.6 %scatter_fusion = f32[192,1792]{0,1:T(8,128)S(1)} fusion(f32[192,1792]{0,1:T(8,128)S(1)} %get-tuple-element.394, s32[2048]{0:T(1024)S(1)} %bitcast.158, f32[2048,192]{1,0:T(8,128)} %copy.151), kind=kCustom, calls=%fused_computation.3.clone.1 | custom fusion | flops 393216 | bytes 4726784 | tf_op jit(solution)/shard_map/while/body/eval_jaxpr/scatter-add | solution.py:58
  134.0 0.8 constant_dynamic-slice_fusion.12
  134.9 1.4 constant_dynamic-slice_fusion.11
  136.3 10.1 %gather_fusion = f32[2048,192]{1,0:T(8,128)} fusion(f32[192,1792]{0,1:T(8,128)} %get-tuple-element.414, s32[2048]{0:T(1024)S(1)} %broadcast_clamp_fusion.2), kind=kCustom, calls=%fused_computation.clone.1 | custom fusion | bytes 3153920 | tf_op jit(solution)/shard_map/while/body/eval_jaxpr/jit(_take)/gather | solution.py:42
  146.3 1.9 copy.147
  148.2 0.6 copy.148
  148.9 1.1 fusion.28
  152.0 0.9 copy.149
  152.9 0.6 copy.150
  153.5 1.8 copy.151
  155.4 12.6 %scatter_fusion = f32[192,1792]{0,1:T(8,128)S(1)} fusion(f32[192,1792]{0,1:T(8,128)S(1)} %get-tuple-element.394, s32[2048]{0:T(1024)S(1)} %bitcast.158, f32[2048,192]{1,0:T(8,128)} %copy.151), kind=kCustom, calls=%fused_computation.3.clone.1 | custom fusion | flops 393216 | bytes 4726784 | tf_op jit(solution)/shard_map/while/body/eval_jaxpr/scatter-add | solution.py:58
  168.1 5.2 %collective-permute-start.4 = (f32[192,256]{0,1:T(8,128)S(1)}, f32[192,256]{0,1:T(8,128)S(1)}, u32[]{:S(2)}, u32[]{:S(2)}) collective-permute-start(f32[192,256]{0,1:T(8,128)S(1)} %get-tuple-element.241), channel_id=1, source_target_pairs={{0,1},{1,2},{2,3},{3,4},{4,5},{5,6},{6,7},{7,8},{8,9},{9,10},{10,1... | collective-permute-start | bytes 589832 | tf_op jit(solution)/shard_map/ppermute | solution.py:16
  173.3 3.1 collective-permute-start.5
  176.4 0.7 fusion.13
  177.1 1.9 collective-permute-start.6
  179.0 5.8 %collective-permute-start.7 = (f32[192,128]{0,1:T(8,128)}, f32[192,128]{0,1:T(8,128)}, u32[]{:S(2)}, u32[]{:S(2)}) collective-permute-start(f32[192,128]{0,1:T(8,128)} %get-tuple-element.240), channel_id=1, source_target_pairs={{32,0},{64,32},{96,64},{128,96},{160,128},{192,160},{224,192},{256... | collective-permute-start | bytes 294920 | tf_op jit(solution)/shard_map/ppermute | solution.py:18
  184.8 1.1 collective-permute-done.5
  185.9 3.7 scatter_custom_fusion.1
  190.1 3.0 scatter_custom_fusion.2
  194.5 0.8 fusion.18
  195.3 55.9 %psum.14 = f32[64,48]{0,1:T(8,128)S(1)} all-reduce(f32[64,48]{0,1:T(8,128)S(1)} %fusion.18), channel_id=1, replica_groups=mesh['sector'=16,'dom'=32] {'sector'}, use_global_device_ids=true, to_apply=%region_15.16 | all-reduce | flops 3072 | bytes 24576 | tf_op jit(solution)/shard_map/psum | solution.py:112
  251.1 148.1 %psum.15 = f32[64,48]{0,1:T(8,128)S(1)} all-reduce(f32[64,48]{0,1:T(8,128)S(1)} %psum.14), channel_id=1, replica_groups=mesh['sector'=16,'dom'=32] {'dom'}, use_global_device_ids=true, to_apply=%region_16.17 | all-reduce | flops 3072 | bytes 24576 | tf_op jit(solution)/shard_map/psum | solution.py:112
  399.2 0.6 broadcast_multiply_fusion.1
  399.8 1.3 copy.92
  (163 shorter events, 13.0 us)
Async XLA Ops:
  0.6 3.4 copy-start
  3.2 0.8 copy-start.2
  6.9 5.2 %copy-start.5 = (s32[2,128]{1,0:T(2,128)S(1)}, s32[2,128]{1,0:T(2,128)}, u32[]{:S(2)}) copy-start(s32[2,128]{1,0:T(2,128)} %param.15) | copy-start | bytes 3076
  7.1 17.2 %collective-permute-start = (f32[192,256]{0,1:T(8,128)S(1)}, f32[192,256]{0,1:T(8,128)S(1)}, u32[]{:S(2)}, u32[]{:S(2)}) collective-permute-start(f32[192,256]{0,1:T(8,128)S(1)} %get-tuple-element.244), channel_id=1, source_target_pairs={{0,1},{1,2},{2,3},{3,4},{4,5},{5,6},{6,7},{7,8},{8,9},{9,10},{10,1... | collective-permute-start | bytes 589832 | tf_op jit(solution)/shard_map/ppermute | solution.py:16
  13.2 17.2 %collective-permute-start.3 = (f32[192,128]{0,1:T(8,128)S(1)}, f32[192,128]{0,1:T(8,128)S(1)}, u32[]{:S(2)}, u32[]{:S(2)}) collective-permute-start(f32[192,128]{0,1:T(8,128)S(1)} %get-tuple-element.245), channel_id=1, source_target_pairs={{32,0},{64,32},{96,64},{128,96},{160,128},{192,160},{224,192},{256... | collective-permute-start | bytes 294920 | tf_op jit(solution)/shard_map/ppermute | solution.py:18
  17.3 13.1 %collective-permute-start.2 = (f32[192,128]{0,1:T(8,128)S(1)}, f32[192,128]{0,1:T(8,128)S(1)}, u32[]{:S(2)}, u32[]{:S(2)}) collective-permute-start(f32[192,128]{0,1:T(8,128)S(1)} %get-tuple-element.246), channel_id=1, source_target_pairs={{0,32},{32,64},{64,96},{96,128},{128,160},{160,192},{192,224},{224... | collective-permute-start | bytes 294920 | tf_op jit(solution)/shard_map/ppermute | solution.py:16
  19.2 11.1 %collective-permute-start.1 = (f32[192,256]{0,1:T(8,128)S(1)}, f32[192,256]{0,1:T(8,128)S(1)}, u32[]{:S(2)}, u32[]{:S(2)}) collective-permute-start(f32[192,256]{0,1:T(8,128)S(1)} %get-tuple-element.243), channel_id=1, source_target_pairs={{1,0},{2,1},{3,2},{4,3},{5,4},{6,5},{7,6},{8,7},{9,8},{10,9},{11,1... | collective-permute-start | bytes 589832 | tf_op jit(solution)/shard_map/ppermute | solution.py:18
  24.3 7.4 %copy-start.4 = (s32[8,1024]{1,0:T(8,128)S(1)}, s32[8,1024]{1,0:T(8,128)}, u32[]{:S(2)}) copy-start(s32[8,1024]{1,0:T(8,128)} %param.13) | copy-start | bytes 98308
  30.4 1.2 copy-start.1
  168.1 16.7 %collective-permute-start.4 = (f32[192,256]{0,1:T(8,128)S(1)}, f32[192,256]{0,1:T(8,128)S(1)}, u32[]{:S(2)}, u32[]{:S(2)}) collective-permute-start(f32[192,256]{0,1:T(8,128)S(1)} %get-tuple-element.241), channel_id=1, source_target_pairs={{0,1},{1,2},{2,3},{3,4},{4,5},{5,6},{6,7},{7,8},{8,9},{9,10},{10,1... | collective-permute-start | bytes 589832 | tf_op jit(solution)/shard_map/ppermute | solution.py:16
  173.3 12.6 %collective-permute-start.5 = (f32[192,256]{0,1:T(8,128)S(1)}, f32[192,256]{0,1:T(8,128)S(1)}, u32[]{:S(2)}, u32[]{:S(2)}) collective-permute-start(f32[192,256]{0,1:T(8,128)S(1)} %get-tuple-element.242), channel_id=1, source_target_pairs={{1,0},{2,1},{3,2},{4,3},{5,4},{6,5},{7,6},{8,7},{9,8},{10,9},{11,1... | collective-permute-start | bytes 589832 | tf_op jit(solution)/shard_map/ppermute | solution.py:18
  177.1 13.0 %collective-permute-start.6 = (f32[192,128]{0,1:T(8,128)}, f32[192,128]{0,1:T(8,128)}, u32[]{:S(2)}, u32[]{:S(2)}) collective-permute-start(f32[192,128]{0,1:T(8,128)} %get-tuple-element.239), channel_id=1, source_target_pairs={{0,32},{32,64},{64,96},{96,128},{128,160},{160,192},{192,224},{224... | collective-permute-start | bytes 294920 | tf_op jit(solution)/shard_map/ppermute | solution.py:16
  179.0 11.1 %collective-permute-start.7 = (f32[192,128]{0,1:T(8,128)}, f32[192,128]{0,1:T(8,128)}, u32[]{:S(2)}, u32[]{:S(2)}) collective-permute-start(f32[192,128]{0,1:T(8,128)} %get-tuple-element.240), channel_id=1, source_target_pairs={{32,0},{64,32},{96,64},{128,96},{160,128},{192,160},{224,192},{256... | collective-permute-start | bytes 294920 | tf_op jit(solution)/shard_map/ppermute | solution.py:18
  193.4 1.1 copy-start.3
